TPU v7x, 32 devices: a whole 2x2x4 slice. The times are simulated.
32 devices in a mesh: seg: 16 (over z, y, x), dir: 2 (over core).
Axes of the slice: x: 2, y: 2, z: 4, core: 2. Of those that a mesh axis runs over, the one named last changes fastest.
Arguments:
- strain: float32 [128, 8, 6, 8192], P('seg'), may hold values from -6 to 6
- valid_flags: int32 [128, 8], P('seg'), may hold values from 0 to 1, as said below
- direction_ids: int32 [1024], P('dir'), may hold values from 0 to 3071
- grid_patterns: float32 [3072, 6], replicated, may hold values from -1 to 1
- grid_delays: float32 [3072, 3], replicated, may hold values from -40 to 40
Outputs:
- peak: float32 [8, 8192], P(None, 'seg')
- dir_score: float32 [8, 1024], P(None, 'dir')
Inputs may be any that keep to these rules, and one draw needn't show every extreme that they name: `valid_flags`: in every draw one window has no usable segment.
All inputs are finite; a program needn't handle non-finite values.
Results may differ from a plain program's by a relative error of at most 0.0001.
Values sent between devices are 32-bit elements; how exact they have to be, the bound alone decides.
No kernel may reach another device: no remote copies, remote signals or barrier semaphores. Data moves between devices by JAX's collectives and lax.ppermute only.
A program may use at most 64 MiB of HBM per device.

v0:
```python
import math
import jax
import jax.numpy as jnp
from jax import lax
from jax.sharding import PartitionSpec as P

F = 8192
PAIRS = ((0, 1), (0, 2), (1, 2))


def spectra(strain, valid_flags):
    weight = valid_flags.astype(jnp.float32)[:, :, None]
    real_part = strain[:, :, 0:3, :]
    imag_part = strain[:, :, 3:6, :]
    parts = []
    for d in range(3):
        parts.append(
            jnp.sum(
                weight
                * (
                    real_part[:, :, d] * real_part[:, :, d]
                    + imag_part[:, :, d] * imag_part[:, :, d]
                ),
                0,
            )
        )
    for d, e in PAIRS:
        parts.append(
            jnp.sum(
                weight
                * (
                    real_part[:, :, d] * real_part[:, :, e]
                    + imag_part[:, :, d] * imag_part[:, :, e]
                ),
                0,
            )
        )
    for d, e in PAIRS:
        parts.append(
            jnp.sum(
                weight
                * (
                    imag_part[:, :, d] * real_part[:, :, e]
                    - real_part[:, :, d] * imag_part[:, :, e]
                ),
                0,
            )
        )
    return jnp.stack(parts, 0)


def null_vectors(rows):
    plus = rows[:, 0:3]
    cross = rows[:, 3:6]
    first = plus[:, 1] * cross[:, 2] - plus[:, 2] * cross[:, 1]
    second = plus[:, 2] * cross[:, 0] - plus[:, 0] * cross[:, 2]
    third = plus[:, 0] * cross[:, 1] - plus[:, 1] * cross[:, 0]
    null = jnp.stack([first, second, third], 1)
    norm2 = jnp.maximum(jnp.sum(null * null, 1), 0.25)
    return (null, norm2)


def project(cov, first_bin, null, norm2, delays, count, total_bins):
    width = cov.shape[2]
    freq = (first_bin + jnp.arange(width, dtype=jnp.int32)).astype(jnp.float32) * (
        2.0 * math.pi / total_bins
    )
    energy = jnp.zeros((null.shape[0], cov.shape[1], width), jnp.float32)
    for d in range(3):
        energy = energy + (null[:, d] * null[:, d])[:, None, None] * cov[d][None]
    for index, (d, e) in enumerate(PAIRS):
        angle = (delays[:, d] - delays[:, e])[:, None] * freq[None, :]
        factor = (2.0 * null[:, d] * null[:, e])[:, None, None]
        energy = energy + factor * (
            jnp.cos(angle)[:, None, :] * cov[3 + index][None]
            + jnp.sin(angle)[:, None, :] * cov[6 + index][None]
        )
    return energy / (norm2[:, None, None] * jnp.maximum(count, 1.0)[None, :, None])


def shards(strain, valid_flags, direction_ids, grid_patterns, grid_delays):
    grid_points = grid_patterns.shape[0]
    one_hot = (direction_ids[:, None] == jnp.arange(grid_points, dtype=jnp.int32)[None, :]).astype(
        jnp.float32
    )
    table = jnp.concatenate([grid_patterns, grid_delays], 1)
    picked = jnp.dot(
        one_hot, table, precision=lax.Precision.HIGHEST, preferred_element_type=jnp.float32
    )
    null, norm2 = null_vectors(picked[:, 0:6])
    delays = picked[:, 6:9]
    count_part = jnp.sum(valid_flags.astype(jnp.float32), 0)
    bin_share = F // lax.axis_size("seg")
    first_bin = lax.axis_index("seg") * bin_share
    cov = lax.psum_scatter(spectra(strain, valid_flags), "seg", scatter_dimension=2, tiled=True)
    count = lax.psum(count_part, "seg")
    power = project(cov, first_bin, null, norm2, delays, count, F)
    peak_part = jnp.max(power, 0)
    score = lax.psum(jnp.sum(power, 2) / F, "seg")
    peak = lax.pmax(peak_part, "dir")
    return (peak, score.T)


def solution(mesh):
    placed = (P("seg", None, None, None), P("seg", None), P("dir"), P(), P())
    return jax.shard_map(
        shards,
        mesh=mesh,
        in_specs=placed,
        out_specs=(P(None, "seg"), P(None, "dir")),
        check_vma=False,
    )
```

profile of v0, /device:TPU:0, one launch (start us, length us, event | category | flops | bytes accessed | tf_op | source)
XLA Modules:
  0.0 199.6 jit_solution(11500045621607774981)
XLA Ops:
  7.2 0.0 reduce-scatter.2.cloned.1.call-start
  7.2 0.7 convert_element_type.12
  7.9 6.5 %fusion.34 = (f32[8,8192]{1,0:T(8,128)S(1)}, f32[8,8192]{1,0:T(8,128)S(1)}, f32[8,8192]{1,0:T(8,128)S(1)}, f32[8,8192]{1,0:T(8,128)S(1)}, f32[8,8192]{1,0:T(8,12...) fusion(f32[8,8,6,8192]{3,1,2,0:T(8,128)} %param.5, ...), kind=kLoop, calls=%fused_computation.48 | loop fusion | flops 23003136 | bytes 14942464 | tf_op jit(solution)/shard_map/reduce_sum | solution.py:40
  14.5 0.0 copy-start.1
  14.5 0.0 copy-start.2
  14.5 0.0 copy-start.3
  14.6 0.0 copy-start.4
  14.7 0.0 copy-start
  14.7 1.4 copy-done
  16.1 0.0 reduce-scatter.2.cloned.1.call-update
  16.1 0.0 copy-done.1
  16.2 43.8 %psum.14 = f32[8]{0:T(128)S(1)} all-reduce(f32[8]{0:T(128)S(1)} %convert_reduce_fusion), channel_id=1, replica_groups=mesh['seg'=16,'dir'=2] {'seg'}, use_global_device_ids=true, to_apply=%region_12.0 | all-reduce | flops 8 | bytes 64 | tf_op jit(solution)/shard_map/psum | solution.py:96
  60.0 0.0 copy-done.2
  60.0 0.0 copy-done.3
  60.0 0.0 copy-done.4
  60.0 3.0 %fusion = f32[512,9]{0,1:T(8,128)S(1)} fusion(s32[512]{0:T(512)S(1)} %copy-done.4, f32[3072,3]{0,1:T(4,128)S(1)} %copy-done.3, f32[3072,6]{0,1:T(8,128)S(1)} %copy-done.2), kind=kOutput, calls=%fused_computation.2 | convolution fusion | flops 171469824 | bytes 131072 | tf_op jit(solution)/shard_map/dot_general | solution.py:87
  63.0 0.1 slice_subtract_fusion.2
  63.1 0.1 broadcast_multiply_fusion
  63.2 12.5 %multiply_cosine_fusion.2 = (f32[512,512]{1,0:T(8,128)S(1)}, f32[512,512]{1,0:T(8,128)S(1)}, f32[512,512]{1,0:T(8,128)S(1)}, f32[512,512]{1,0:T(8,128)}, f32[512,512]{1,0:T(8,128)}, /*index=5*/f32[512,512]{1,0:T(8,128)}) fusion(f32[512]{0:T(512)S(1)} %convert_multiply_fusion, f32[512]{0:T(512)S(1)} %bitcast.242, f32[512]{0:T(512)S(1)} %bitcast.243, ...), kind=kLoop, calls=%fused_computation.63 | loop fusion | flops 786432 | bytes 6299648 | tf_op jit(solution)/shard_map/cos | solution.py:75
  75.7 25.3 %reduce-scatter.2.cloned.1.call-done = f32[9,8,512]{2,1,0:T(8,128)} async-done(((f32[9,8,8192]{2,1,0:T(8,128)}), f32[9,8,512]{2,1,0:T(8,128)}) %reduce-scatter.2.cloned.1.call-update) | async-done | bytes 147472 | tf_op jit(solution)/shard_map/reduce_scatter | solution.py:95
  101.0 0.9 slice_bitcast_fusion.8
  101.9 10.6 %fusion.44 = (f32[512,8]{1,0:T(8,128)S(1)}, f32[8,512]{1,0:T(8,128)S(1)}) fusion(f32[512,8]{1,0:T(8,128)S(1)} %broadcast_multiply_fusion, f32[8,512]{1,0:T(8,128)S(1)} %get-tuple-element.23, f32[512,512]{1,0:T(8,128)} %get-tuple-element.51, f32[8,512]{1,0:T(8,128)S(1)} %get-tuple-element.24, f32[512,512]{1,0:T(8,128)} %get-tuple-element.52, ...), kind=kLoop, calls=%fused_computation.102 | loop fusion | flops 48226304 | bytes 6500352 | tf_op jit(solution)/shard_map/reduce_sum | solution.py:99
  112.5 75.6 %psum.15 = f32[8,512]{0,1:T(8,128)S(1)} all-reduce(f32[8,512]{0,1:T(8,128)S(1)} %multiply_bitcast_fusion), channel_id=1, replica_groups=mesh['seg'=16,'dir'=2] {'seg'}, use_global_device_ids=true, to_apply=%region_16.0 | all-reduce | flops 4096 | bytes 32768 | tf_op jit(solution)/shard_map/psum | solution.py:99
  188.1 0.7 copy.31
  188.8 3.9 %pmax.7 = f32[8,512]{1,0:T(8,128)} all-reduce(f32[8,512]{1,0:T(8,128)S(1)} %get-tuple-element.14), channel_id=1, replica_groups=mesh['seg'=16,'dir'=2] {'dir'}, use_global_device_ids=true, to_apply=%region_14.0 | all-reduce | flops 4096 | bytes 32768 | tf_op jit(solution)/shard_map/pmax | solution.py:100
  (17 shorter events, 0.3 us)
Async XLA Ops:
  7.2 93.9 %reduce-scatter.2.cloned.1.call-start = ((), (), s32[]{:S(2)}) async-start(), calls=%async_computation.1 | async-start | bytes 2506752 | tf_op jit(solution)/shard_map/reduce_scatter | solution.py:95
  14.5 1.6 copy-start.1
  14.5 45.4 %copy-start.2 = (f32[3072,6]{0,1:T(8,128)S(1)}, f32[3072,6]{0,1:T(8,128)}, u32[]{:S(2)}) copy-start(f32[3072,6]{0,1:T(8,128)} %param.8) | copy-start | bytes 221188
  14.5 45.4 %copy-start.3 = (f32[3072,3]{0,1:T(4,128)S(1)}, f32[3072,3]{0,1:T(4,128)}, u32[]{:S(2)}) copy-start(f32[3072,3]{0,1:T(4,128)} %param.9) | copy-start | bytes 110596
  14.6 45.4 %copy-start.4 = (s32[512]{0:T(512)S(1)}, s32[512]{0:T(512)}, u32[]{:S(2)}) copy-start(s32[512]{0:T(512)} %param.7) | copy-start | bytes 6148
  14.7 1.4 copy-start
Sparse Core Ops, SparseCore 0:
  16.2 84.7 reduce-scatter.1
where the time goes:
time: 200 us
  blocking collectives  123 us (62%)
  other arithmetic  30.5 us (15%)
  waiting for transfers between devices  25.3 us (13%)
  between operations  14.2 us (7%)
  local copies, waits for them, and re-layouts  3.19 us (2%)
  matrix products  2.97 us (1%)
    psum x1, blocking collectives, shards(): score = lax.psum(jnp.sum(power, 2) / F, 'seg')  75.6 us
    psum x1, blocking collectives, shards(): count = lax.psum(count_part, 'seg')  43.8 us
    reduce_scatter x1, waiting for transfers between devices, shards(): lax.psum_scatter(spectra(strain, valid_flags), 'seg', scatter_dimension=2...  25.3 us
    cos x1, other arithmetic, project(): jnp.cos(angle)[:, None, :] * cov[3 + index][None]  12.5 us
    reduce_sum x1, other arithmetic, shards(): score = lax.psum(jnp.sum(power, 2) / F, 'seg')  10.6 us
    reduce_sum x1, other arithmetic, spectra(): jnp.sum(weight * (imag_part[:, :, d] * real_part[:, :, e] - real_part[:,...  6.48 us
  transfers between devices with their start and end apart: 1, of which 1 were waited for; matrix products, arithmetic and copies ran while one was open for 8% of the time, Pallas kernels for 0%

commit v1 on v0

--- a/solution.py
+++ b/solution.py
@@ -96,7 +96,7 @@
     count = lax.psum(count_part, "seg")
     power = project(cov, first_bin, null, norm2, delays, count, F)
     peak_part = jnp.max(power, 0)
-    score = lax.psum(jnp.sum(power, 2) / F, "seg")
+    score = jnp.sum(jax.lax.all_gather(jnp.sum(power, 2) / F, "seg"), axis=0)
     peak = lax.pmax(peak_part, "dir")
     return (peak, score.T)
 

time: 200 us -> 164 us (0.82)
  blocking collectives: 123 us -> 86 us
    psum x1 -> x0, blocking collectives: 75.6 us -> none  [shards(): score = lax.psum(jnp.sum(power, 2) / F, 'seg')]
    all_gather x0 -> x1, blocking collectives: none -> 38.2 us  [shards(): score = jnp.sum(jax.lax.all_gather(jnp.sum(power, 2) / F, 'seg'), axis=0)]
    reduce_sum x1 -> x2, other arithmetic: 10.6 us -> 11.9 us  [shards(): score = jnp.sum(jax.lax.all_gather(jnp.sum(power, 2) / F, 'seg'), axis=0)]
  transfers between devices with their start and end apart: 1 -> 1, of which waited for: 1 -> 1; matrix products, arithmetic and copies ran while one was open for 8% -> 10% of each run, Pallas kernels for 0% -> 0%
where the time goes in v1:
time: 164 us
  blocking collectives  86 us (52%)
  other arithmetic  31.8 us (19%)
  waiting for transfers between devices  25.3 us (15%)
  between operations  14.2 us (9%)
  local copies, waits for them, and re-layouts  3.52 us (2%)
  matrix products  2.97 us (2%)
    psum x1, blocking collectives, shards(): count = lax.psum(count_part, 'seg')  43.8 us
    all_gather x1, blocking collectives, shards(): score = jnp.sum(jax.lax.all_gather(jnp.sum(power, 2) / F, 'seg'), axis=0)  38.2 us
    reduce_scatter x1, waiting for transfers between devices, shards(): lax.psum_scatter(spectra(strain, valid_flags), 'seg', scatter_dimension=2...  25.3 us
    cos x1, other arithmetic, project(): jnp.cos(angle)[:, None, :] * cov[3 + index][None]  12.5 us
    reduce_sum x2, other arithmetic, shards(): score = jnp.sum(jax.lax.all_gather(jnp.sum(power, 2) / F, 'seg'), axis=0)  11.9 us
    reduce_sum x1, other arithmetic, spectra(): jnp.sum(weight * (imag_part[:, :, d] * real_part[:, :, e] - real_part[:,...  6.48 us
    pmax x1, blocking collectives, shards(): peak = lax.pmax(peak_part, 'dir')  3.94 us
  transfers between devices with their start and end apart: 1, of which 1 were waited for; matrix products, arithmetic and copies ran while one was open for 10% of the time, Pallas kernels for 0%

profile of v1, /device:TPU:0, one launch (start us, length us, event | category | flops | bytes accessed | tf_op | source)
XLA Modules:
  0.0 163.9 jit_solution(3993309659040922456)
XLA Ops:
  7.2 0.0 reduce-scatter.2.cloned.1.call-start
  7.2 0.7 convert_element_type.12
  7.9 6.5 %fusion.34 = (f32[8,8192]{1,0:T(8,128)S(1)}, f32[8,8192]{1,0:T(8,128)S(1)}, f32[8,8192]{1,0:T(8,128)S(1)}, f32[8,8192]{1,0:T(8,128)S(1)}, f32[8,8192]{1,0:T(8,12...) fusion(f32[8,8,6,8192]{3,1,2,0:T(8,128)} %param.5, ...), kind=kLoop, calls=%fused_computation.48 | loop fusion | flops 23003136 | bytes 14942464 | tf_op jit(solution)/shard_map/reduce_sum | solution.py:40
  14.5 0.0 copy-start.1
  14.5 0.0 copy-start.2
  14.5 0.0 copy-start.3
  14.6 0.0 copy-start.4
  14.7 0.0 copy-start
  14.7 1.4 copy-done
  16.1 0.0 reduce-scatter.2.cloned.1.call-update
  16.1 0.0 copy-done.1
  16.2 43.8 %psum.7 = f32[8]{0:T(128)S(1)} all-reduce(f32[8]{0:T(128)S(1)} %convert_reduce_fusion), channel_id=1, replica_groups=mesh['seg'=16,'dir'=2] {'seg'}, use_global_device_ids=true, to_apply=%region_12.0 | all-reduce | flops 8 | bytes 64 | tf_op jit(solution)/shard_map/psum | solution.py:96
  60.0 0.0 copy-done.2
  60.0 0.0 copy-done.3
  60.0 0.0 copy-done.4
  60.0 3.0 %fusion = f32[512,9]{0,1:T(8,128)S(1)} fusion(s32[512]{0:T(512)S(1)} %copy-done.4, f32[3072,3]{0,1:T(4,128)S(1)} %copy-done.3, f32[3072,6]{0,1:T(8,128)S(1)} %copy-done.2), kind=kOutput, calls=%fused_computation.2 | convolution fusion | flops 171469824 | bytes 131072 | tf_op jit(solution)/shard_map/dot_general | solution.py:87
  63.0 0.1 slice_subtract_fusion.2
  63.1 0.1 broadcast_multiply_fusion
  63.2 12.5 %multiply_cosine_fusion.2 = (f32[512,512]{1,0:T(8,128)S(1)}, f32[512,512]{1,0:T(8,128)S(1)}, f32[512,512]{1,0:T(8,128)S(1)}, f32[512,512]{1,0:T(8,128)}, f32[512,512]{1,0:T(8,128)}, /*index=5*/f32[512,512]{1,0:T(8,128)}) fusion(f32[512]{0:T(512)S(1)} %convert_multiply_fusion, f32[512]{0:T(512)S(1)} %bitcast.244, f32[512]{0:T(512)S(1)} %bitcast.245, ...), kind=kLoop, calls=%fused_computation.63 | loop fusion | flops 786432 | bytes 6299648 | tf_op jit(solution)/shard_map/cos | solution.py:75
  75.7 25.3 %reduce-scatter.2.cloned.1.call-done = f32[9,8,512]{2,1,0:T(8,128)} async-done(((f32[9,8,8192]{2,1,0:T(8,128)}), f32[9,8,512]{2,1,0:T(8,128)}) %reduce-scatter.2.cloned.1.call-update) | async-done | bytes 147472 | tf_op jit(solution)/shard_map/reduce_scatter | solution.py:95
  101.0 0.9 slice_bitcast_fusion.8
  101.9 11.3 %fusion.44 = (f32[512,8]{1,0:T(8,128)}, f32[8,512]{1,0:T(8,128)S(1)}) fusion(f32[512,8]{1,0:T(8,128)S(1)} %broadcast_multiply_fusion, f32[8,512]{1,0:T(8,128)S(1)} %get-tuple-element.21, f32[512,512]{1,0:T(8,128)} %get-tuple-element.49, f32[8,512]{1,0:T(8,128)S(1)} %get-tuple-element.22, f32[512,512]{1,0:T(8,128)} %get-tuple-element.50, ...), kind=kLoop, calls=%fused_computation.102 | loop fusion | flops 48226304 | bytes 6500352 | tf_op jit(solution)/shard_map/reduce_sum | solution.py:99
  113.2 1.0 copy.44
  114.2 38.2 %all-gather = f32[8192,8]{0,1:T(8,128)S(1)} all-gather(f32[512,8]{0,1:T(8,128)S(1)} %broadcast_multiply_fusion.1), channel_id=2, replica_groups=mesh['seg'=16,'dir'=2] {'seg'}, dimensions={0}, use_global_device_ids=true | all-gather | bytes 278528 | tf_op jit(solution)/shard_map/all_gather | solution.py:99
  152.5 3.9 %pmax.7 = f32[8,512]{1,0:T(8,128)} all-reduce(f32[8,512]{1,0:T(8,128)S(1)} %get-tuple-element.12), channel_id=1, replica_groups=mesh['seg'=16,'dir'=2] {'dir'}, use_global_device_ids=true, to_apply=%region_14.0 | all-reduce | flops 4096 | bytes 32768 | tf_op jit(solution)/shard_map/pmax | solution.py:100
  156.4 0.6 reduce_sum.129
  (17 shorter events, 0.3 us)
Async XLA Ops:
  7.2 93.9 %reduce-scatter.2.cloned.1.call-start = ((), (), s32[]{:S(2)}) async-start(), calls=%async_computation.1 | async-start | bytes 2506752 | tf_op jit(solution)/shard_map/reduce_scatter | solution.py:95
  14.5 1.6 copy-start.1
  14.5 45.4 %copy-start.2 = (f32[3072,6]{0,1:T(8,128)S(1)}, f32[3072,6]{0,1:T(8,128)}, u32[]{:S(2)}) copy-start(f32[3072,6]{0,1:T(8,128)} %param.8) | copy-start | bytes 221188
  14.5 45.4 %copy-start.3 = (f32[3072,3]{0,1:T(4,128)S(1)}, f32[3072,3]{0,1:T(4,128)}, u32[]{:S(2)}) copy-start(f32[3072,3]{0,1:T(4,128)} %param.9) | copy-start | bytes 110596
  14.6 45.4 %copy-start.4 = (s32[512]{0:T(512)S(1)}, s32[512]{0:T(512)}, u32[]{:S(2)}) copy-start(s32[512]{0:T(512)} %param.7) | copy-start | bytes 6148
  14.7 1.4 copy-start
Sparse Core Ops, SparseCore 0:
  16.2 84.7 reduce-scatter.1
